TPU v7x, 256 devices: a whole 4x4x8 slice. The times are simulated.
256 devices in a mesh: lat: 8 (over z_hi, core), lon: 32 (over x, z_lo, y).
Axes of the slice: x: 4, y: 4, z: 8 (z_hi: 4, z_lo: 2; z = z_hi * 2 + z_lo), core: 2. Of those that a mesh axis runs over, the one named last changes fastest.
Arguments:
- forcing: bfloat16 [16, 128, 4096], P(None, 'lat', 'lon'), may hold values from -6 to 6
- hidden: bfloat16 [64, 128, 4096], P(None, 'lat', 'lon'), may hold values from -3 to 3
- cell: bfloat16 [64, 128, 4096], P(None, 'lat', 'lon'), may hold values from -6 to 6
- grad_hidden: bfloat16 [64, 128, 4096], P(None, 'lat', 'lon'), may hold values from -6 to 6
- grad_cell: bfloat16 [64, 128, 4096], P(None, 'lat', 'lon'), may hold values from -6 to 6
- wet_mask: int32 [8, 256], P('lat'), may hold values from 0 to 1
- tile_owner: int32 [8, 256], P('lat'), may hold values from 0 to 31, as said below
- w_gates: bfloat16 [256, 720], replicated, may hold values from -0.21875 to 0.21875
- b_gates: float32 [256], replicated, may hold values from -3 to 3
Outputs:
- hidden_next: bfloat16 [64, 128, 4096], P(None, 'lat', 'lon')
- cell_next: float32 [1024, 64, 256], P(('lat', 'lon'))
- hidden_grad: float32 [64, 128, 4096], P(None, 'lat', 'lon')
- cell_grad: float32 [64, 128, 4096], P(None, 'lat', 'lon')
- weight_grad: float32 [256, 720], replicated
- bias_grad: float32 [256], replicated
Inputs may be any that keep to these rules, and one draw needn't show every extreme that they name: Within each group of 1 tile rows, tile_owner gives every longitude index exactly 4 wet tiles, and gives the wet tiles of one longitude block of 8 tile columns at most 1 to any one index; both bounds are reached in every draw, and some block is wet throughout. Dry tiles carry an owner too.
All inputs are finite; a program needn't handle non-finite values.
Results may differ from a plain program's by a relative error of at most 0.0033.
Values may be sent and summed in bfloat16 or wider, within the bound.
A program may use at most 64 MiB of HBM per device.

v0:
```python
import math
import jax
import jax.numpy as jnp
from jax import lax
from jax.sharding import PartitionSpec as P

TILE = 16


def extended_2(cells, sides, width):
    for axis, dim in sides:
        count = lax.axis_size(axis)
        head = lax.slice_in_dim(cells, 0, width, axis=dim)
        tail = lax.slice_in_dim(cells, cells.shape[dim] - width, cells.shape[dim], axis=dim)
        cells = jnp.concatenate(
            [
                lax.ppermute(tail, axis, [(i, (i + 1) % count) for i in range(count)]),
                cells,
                lax.ppermute(head, axis, [((i + 1) % count, i) for i in range(count)]),
            ],
            axis=dim,
        )
    return cells


def last_pad(values_in, pad_front, pad_back):
    widths = [(0, 0)] * (values_in.ndim - 1) + [(pad_front, pad_back)]
    return jnp.pad(values_in, widths)


def fold_edges(values_in):
    tile_count = values_in.shape[-2]
    inner_size = values_in.shape[-1] - 2
    leading = values_in.shape[:-2]
    flat_shape = leading + (tile_count * inner_size,)
    middle = values_in[..., 1 : inner_size + 1].reshape(flat_shape)
    zeros_left = jnp.zeros(leading + (tile_count, inner_size - 1), values_in.dtype)
    left_edge = jnp.concatenate([values_in[..., 0:1], zeros_left], -1).reshape(flat_shape)
    zeros_one = jnp.zeros(leading + (tile_count, 1), values_in.dtype)
    zeros_rest = jnp.zeros(leading + (tile_count, inner_size - 2), values_in.dtype)
    right_edge = jnp.concatenate(
        [zeros_one, values_in[..., inner_size + 1 : inner_size + 2], zeros_rest], -1
    ).reshape(flat_shape)
    full_size = tile_count * inner_size + 2
    return (
        last_pad(middle, 1, 1)
        + last_pad(left_edge, 0, 2)
        + last_pad(right_edge, inner_size, 0)[..., :full_size]
    )


def lstm_terms(pre_in, pre_forget, pre_out, pre_cand, cell_in, hidden_cot, cell_cot, live_cells):
    gate_in = jax.nn.sigmoid(pre_in)
    gate_forget = jax.nn.sigmoid(pre_forget)
    gate_out = jax.nn.sigmoid(pre_out)
    candidate = jnp.tanh(pre_cand)
    cell_new = gate_forget * cell_in + gate_in * candidate
    squash = jnp.tanh(cell_new)
    hidden_new = (live_cells * gate_out * squash).astype(jnp.bfloat16)
    back_h = live_cells * hidden_cot.astype(jnp.float32)
    back_c = live_cells * cell_cot.astype(jnp.float32) + back_h * gate_out * (1.0 - squash * squash)
    cell_back = back_c * gate_forget
    delta_parts = (
        back_c * candidate * gate_in * (1.0 - gate_in),
        back_c * cell_in * gate_forget * (1.0 - gate_forget),
        back_h * squash * gate_out * (1.0 - gate_out),
        back_c * gate_in * (1.0 - candidate * candidate),
    )
    return (hidden_new, cell_new, cell_back, delta_parts)


def tile_step(slab_tiles, cell_tiles, hidden_cot, cell_cot, live_tiles, w_gates, b_gates):
    tile_count = slab_tiles.shape[0]
    channels = slab_tiles.shape[1]
    hid_count = cell_tiles.shape[1]
    side_cells = TILE
    tile_grid = slab_tiles.reshape(tile_count, channels, side_cells + 2, side_cells + 2)
    tap_list = []
    for row_off in range(3):
        for col_off in range(3):
            tap_list.append(
                tile_grid[
                    :, :, row_off : row_off + side_cells, col_off : col_off + side_cells
                ].reshape(tile_count, channels, side_cells * side_cells)
            )
    patches = jnp.concatenate(tap_list, 1)
    pre_gates = (
        jnp.einsum("gk,nkc->ngc", w_gates, patches, preferred_element_type=jnp.float32)
        + b_gates[None, :, None]
    )
    live_cells = live_tiles[:, None, None]
    hidden_new, cell_new, cell_back, delta_parts = lstm_terms(
        pre_gates[:, :hid_count],
        pre_gates[:, hid_count : 2 * hid_count],
        pre_gates[:, 2 * hid_count : 3 * hid_count],
        pre_gates[:, 3 * hid_count :],
        cell_tiles.astype(jnp.float32),
        hidden_cot,
        cell_cot,
        live_cells,
    )
    gate_delta = jnp.concatenate(delta_parts, 1).astype(jnp.bfloat16)
    weight_part = jnp.einsum("ngc,nkc->gk", gate_delta, patches, preferred_element_type=jnp.float32)
    bias_part = jnp.sum(gate_delta.astype(jnp.float32), axis=(0, 2))
    hid_weights = w_gates.reshape(w_gates.shape[0], 9, channels)[:, :, channels - hid_count :]
    spread = jnp.einsum(
        "gth,ngc->nthc", hid_weights, gate_delta, preferred_element_type=jnp.float32
    )
    grad_pad = jnp.zeros((tile_count, hid_count, side_cells + 2, side_cells + 2), jnp.float32)
    for row_off in range(3):
        for col_off in range(3):
            placed = spread[:, row_off * 3 + col_off].reshape(
                tile_count, hid_count, side_cells, side_cells
            )
            grad_pad = grad_pad + jnp.pad(
                placed, ((0, 0), (0, 0), (row_off, 2 - row_off), (col_off, 2 - col_off))
            )
    grad_pad = grad_pad.reshape(tile_count, hid_count, (side_cells + 2) * (side_cells + 2))
    return (hidden_new, cell_new, cell_back, grad_pad, weight_part, bias_part)


def outside_rows(row_total, lat_index, lat_devices):
    position = jnp.arange(row_total, dtype=jnp.int32)
    upper = (position == 0) & (lat_index == 0)
    lower = (position == row_total - 1) & (lat_index == lat_devices - 1)
    return jnp.where(upper | lower, 0.0, 1.0).astype(jnp.float32)


def cut_tiles(padded, tile_rows, tile_cols):
    channels = padded.shape[0]
    side_cells = TILE + 2
    row_pick = (
        jnp.arange(tile_rows, dtype=jnp.int32)[:, None] * TILE
        + jnp.arange(side_cells, dtype=jnp.int32)[None, :]
    ).reshape(-1)
    col_pick = (
        jnp.arange(tile_cols, dtype=jnp.int32)[:, None] * TILE
        + jnp.arange(side_cells, dtype=jnp.int32)[None, :]
    ).reshape(-1)
    strips = jnp.take(padded, row_pick, axis=1).reshape(
        channels, tile_rows, side_cells, padded.shape[2]
    )
    pieces = jnp.take(strips, col_pick, axis=3).reshape(
        channels, tile_rows, side_cells, tile_cols, side_cells
    )
    return jnp.transpose(pieces, (1, 3, 0, 2, 4)).reshape(
        tile_rows * tile_cols, channels, side_cells * side_cells
    )


def to_tiles(values_in, tile_rows, tile_cols):
    channels = values_in.shape[0]
    shaped = values_in.reshape(channels, tile_rows, TILE, tile_cols, TILE)
    return jnp.transpose(shaped, (1, 3, 0, 2, 4)).reshape(
        tile_rows * tile_cols, channels, TILE * TILE
    )


def from_tiles(tiles_in, tile_rows, tile_cols):
    channels = tiles_in.shape[1]
    shaped = tiles_in.reshape(tile_rows, tile_cols, channels, TILE, TILE)
    return jnp.transpose(shaped, (2, 0, 3, 1, 4)).reshape(
        channels, tile_rows * TILE, tile_cols * TILE
    )


def sender_plan(wet_local, dest_local, slot_count, pair_most):
    tile_count = wet_local.shape[0]
    position = jnp.arange(tile_count, dtype=jnp.int32)
    earlier = position[:, None] < position[None, :]
    same_dest = (
        (dest_local[:, None] == dest_local[None, :]) & wet_local[:, None] & wet_local[None, :]
    )
    dest_rank = jnp.sum((same_dest & earlier).astype(jnp.int32), 0)
    slot_of = dest_local * pair_most + dest_rank
    placed = wet_local[:, None] & (
        slot_of[:, None] == jnp.arange(slot_count, dtype=jnp.int32)[None, :]
    )
    source = jnp.sum(placed.astype(jnp.int32) * position[:, None], 0)
    filled = jnp.any(placed, 0)
    send_index = jnp.where(filled, source, tile_count)
    home_index = jnp.where(wet_local, slot_of, slot_count)
    return (send_index, home_index)


def receiver_plan(arrivals, pair_most, capacity):
    slot_count = arrivals.shape[0] * pair_most
    positions = jnp.arange(slot_count, dtype=jnp.int32)
    filled = positions % pair_most < jnp.repeat(arrivals, pair_most)
    slot_rank = jnp.cumsum(filled.astype(jnp.int32)) - 1
    placed = filled[None, :] & (
        slot_rank[None, :] == jnp.arange(capacity, dtype=jnp.int32)[:, None]
    )
    work_index = jnp.sum(placed.astype(jnp.int32) * positions[None, :], 1)
    back_index = jnp.where(filled, slot_rank, capacity)
    return (work_index, back_index)


def pick_rows(arrays, row_index):
    picked = []
    for member in arrays:
        extended = jnp.concatenate([member, jnp.zeros((1,) + member.shape[1:], member.dtype)], 0)
        picked.append(jnp.take(extended, row_index, axis=0))
    return tuple(picked)


def fold_grad(pad_tiles, tile_rows, tile_cols, row_keep):
    hid_count = pad_tiles.shape[1]
    side_cells = TILE + 2
    shaped = pad_tiles.reshape(tile_rows, tile_cols, hid_count, side_cells, side_cells)
    across = fold_edges(jnp.transpose(shaped, (0, 2, 3, 1, 4)))
    down_fold = fold_edges(jnp.transpose(across, (1, 3, 0, 2)))
    overhang = jnp.transpose(down_fold, (0, 2, 1)) * row_keep[None, :, None]
    received = extended_2(overhang, (("lat", 1), ("lon", 2)), 1)
    lat_size = overhang.shape[1] - 2
    lon_size = overhang.shape[2] - 2
    columns = received[:, :, 2 : lon_size + 2]
    columns = columns.at[:, :, 0].add(received[:, :, 0])
    columns = columns.at[:, :, lon_size - 1].add(received[:, :, lon_size + 3])
    result = columns[:, 2 : lat_size + 2]
    result = result.at[:, 0].add(columns[:, 0])
    result = result.at[:, lat_size - 1].add(columns[:, lat_size + 3])
    return result


def body(forcing, hidden, cell, grad_hidden, grad_cell, wet_mask, tile_owner, w_gates, b_gates):
    lat_index = lax.axis_index("lat")
    lon_index = lax.axis_index("lon")
    lat_devices = lax.axis_size("lat")
    lon_devices = lax.axis_size("lon")
    tile_rows = wet_mask.shape[0]
    tile_cols = wet_mask.shape[1] // lon_devices
    tile_count = tile_rows * tile_cols
    pair_most = max(1, tile_count // lon_devices)
    slot_count = lon_devices * pair_most
    capacity = tile_count // 2
    fields = jnp.concatenate([forcing, hidden], 0)
    padded = extended_2(fields, (("lat", 1), ("lon", 2)), 1)
    row_keep = outside_rows(padded.shape[1], lat_index, lat_devices)
    padded = padded * row_keep.astype(jnp.bfloat16)[None, :, None]
    slab_tiles = cut_tiles(padded, tile_rows, tile_cols)
    cell_tiles = to_tiles(cell, tile_rows, tile_cols)
    hidden_cot = to_tiles(grad_hidden, tile_rows, tile_cols)
    cell_cot = to_tiles(grad_cell, tile_rows, tile_cols)
    wet_local = (
        lax.dynamic_slice_in_dim(wet_mask, lon_index * tile_cols, tile_cols, 1).reshape(tile_count)
        > 0
    )
    dest_local = lax.dynamic_slice_in_dim(tile_owner, lon_index * tile_cols, tile_cols, 1).reshape(
        tile_count
    )
    send_index, home_index = sender_plan(wet_local, dest_local, slot_count, pair_most)
    owned_here = (wet_mask > 0) & (tile_owner == lon_index)
    arrivals = jnp.sum(
        owned_here.reshape(tile_rows, lon_devices, tile_cols).astype(jnp.int32), axis=(0, 2)
    )
    work_index, back_index = receiver_plan(arrivals, pair_most, capacity)
    hid_tiles, cell_new, back_tiles, pad_tiles, weight_part, bias_part = tile_step(
        slab_tiles,
        cell_tiles,
        hidden_cot,
        cell_cot,
        wet_local.astype(jnp.float32),
        w_gates,
        b_gates,
    )
    outgoing_state = pick_rows((cell_new,), send_index)[0]
    incoming_state = lax.all_to_all(outgoing_state, "lon", split_axis=0, concat_axis=0, tiled=True)
    cell_next = pick_rows((incoming_state,), work_index)[0]
    hidden_next = from_tiles(hid_tiles, tile_rows, tile_cols)
    cell_grad = from_tiles(back_tiles, tile_rows, tile_cols)
    hidden_grad = fold_grad(pad_tiles, tile_rows, tile_cols, row_keep)
    totals = lax.psum((weight_part, bias_part), ("lat", "lon"))
    scaling = 1.0 / math.sqrt(float(lat_devices * lon_devices * capacity * TILE * TILE))
    return (
        hidden_next,
        cell_next,
        hidden_grad,
        cell_grad,
        totals[0] * scaling,
        totals[1] * scaling,
    )


def solution(mesh):
    return jax.shard_map(
        body,
        mesh=mesh,
        in_specs=(
            P(None, "lat", "lon"),
            P(None, "lat", "lon"),
            P(None, "lat", "lon"),
            P(None, "lat", "lon"),
            P(None, "lat", "lon"),
            P("lat", None),
            P("lat", None),
            P(),
            P(),
        ),
        out_specs=(
            P(None, "lat", "lon"),
            P(("lat", "lon"), None, None),
            P(None, "lat", "lon"),
            P(None, "lat", "lon"),
            P(),
            P(),
        ),
        check_vma=False,
    )
```

profile of v0, /device:TPU:6, one launch (start us, length us, event | category | flops | bytes accessed | tf_op | source)
XLA Modules:
  0.0 355.3 jit_solution(3883284366061151006)
XLA Ops:
  9.9 5.8 %collective-permute-start.1 = (bf16[80,1,128]{0,2,1:T(8,128)(2,1)S(1)}, bf16[80,1,128]{0,2,1:T(8,128)(2,1)S(1)}, u32[]{:S(2)}, u32[]{:S(2)}) collective-permute-start(bf16[80,1,128]{0,2,1:T(8,128)(2,1)S(1)} %get-tuple-element.100), channel_id=1, source_target_pairs={{32,0},{64,32},{96,64},{128,96},{160,128},{192,160},{224,192},{0,2... | collective-permute-start | bytes 61448 | tf_op jit(solution)/shard_map/ppermute | solution.py:19
  21.4 1.7 collective-permute-start.2
  23.1 3.5 collective-permute-start.3
  27.7 1.5 copy.101
  29.3 2.3 copy.109
  31.6 1.5 copy.110
  34.2 2.4 copy.107
  39.1 2.0 fusion.35
  43.2 1.9 copy.88
  45.0 2.0 copy.97
  47.0 1.9 copy.87
  48.9 2.0 copy.96
  50.8 1.9 copy.86
  52.7 2.0 copy.95
  54.6 1.9 copy.85
  56.5 2.0 copy.94
  59.3 2.0 copy.93
  68.3 1.4 fusion.29
  69.8 1.5 multiply_convert_fusion.3
  71.2 1.8 convolution_bitcast_fusion.1
  73.8 1.6 broadcast_select_fusion
  75.4 5.6 %all-to-all-start = ((f32[32,64,256]{2,1,0:T(8,128)}), f32[32,64,256]{2,1,0:T(8,128)S(1)}, u32[]{:S(2)}, u32[]{:S(2)}) async-start(f32[32,64,256]{2,1,0:T(8,128)} %broadcast_select_fusion), calls=%async_computation | async-start | bytes 4194304 | tf_op jit(solution)/shard_map/all_to_all | solution.py:268
  81.0 1.7 convolution_bitcast_fusion
  82.8 2.2 fusion.32
  86.4 2.3 copy.120
  88.7 2.4 copy.119
  91.1 2.4 copy.118
  93.5 2.4 copy.117
  95.9 2.4 copy.116
  98.3 2.4 copy.115
  100.7 2.4 copy.114
  103.1 2.4 copy.113
  105.5 4.7 %add_bitcast_fusion.1 = f32[1,64,18,8,18]{1,4,2,3,0:T(8,128)S(1)} fusion(f32[8,64,16,16]{1,3,2,0:T(8,128)} %bitcast.122, f32[8,64,16,16]{1,3,2,0:T(8,128)} %bitcast.123, f32[8,64,16,16]{1,3,2,0:T(8,128)} %bitcast.124, f32[8,64,16,16]{1,3,2,0:T(8,128)} %bitcast.125, f32[8,64,16,16]{1,3,2,0:T(8,128)} %bitcast.126, f32[8,64,16,16]{1,3,2,0:T(8,128)} %bitcast.127, ...), kind=kLoop, calls=%fused_computation.8 | loop fusion | flops 1327104 | bytes 5382144 | tf_op jit(solution)/shard_map/transpose | solution.py:211
  112.5 3.9 %collective-permute-start.5 = (f32[64,1,130]{0,2,1:T(8,128)}, f32[64,1,130]{0,2,1:T(8,128)S(1)}, u32[]{:S(2)}, u32[]{:S(2)}) collective-permute-start(f32[64,1,130]{0,2,1:T(8,128)} %get-tuple-element.94), channel_id=1, source_target_pairs={{32,0},{64,32},{96,64},{128,96},{160,128},{192,160},{224,192},{0,2... | collective-permute-start | bytes 99848 | tf_op jit(solution)/shard_map/ppermute | solution.py:19
  116.6 75.5 %psum.15 = f32[256]{0:T(256)S(1)} all-reduce(f32[256]{0:T(256)S(1)} %convert_reduce_fusion), channel_id=1, replica_groups=mesh['lat'=8,'lon'=32] {'lat','lon'}, use_global_device_ids=true, to_apply=%region_8.9 | all-reduce | flops 256 | bytes 2048 | tf_op jit(solution)/shard_map/psum | solution.py:273
  192.7 2.0 copy.102
  194.6 1.9 copy.103
  196.5 2.0 copy.126
  198.5 2.3 copy.124
  200.9 2.4 copy.125
  203.2 2.4 copy.128
  209.0 4.0 %collective-permute-done.6 = f32[64,20,1]{0,2,1:T(1,128)S(1)} collective-permute-done((f32[64,20,1]{0,2,1:T(1,128)S(1)}, f32[64,20,1]{0,2,1:T(1,128)S(1)}, u32[]{:S(2)}, u32[]{:S(2)}) %collective-permute-start.6) | collective-permute-done | bytes 5152 | tf_op jit(solution)/shard_map/ppermute | solution.py:17
  213.1 1.6 scatter-add.14
  215.6 1.6 scatter-add.15
  221.4 120.5 %all-reduce.19.cloned.1.call-done = f32[256,720]{0,1:T(8,128)} async-done(((f32[256,720]{0,1:T(8,128)}), f32[256,720]{0,1:T(8,128)}) %all-reduce.19.cloned.1.call-update) | async-done | bytes 737296 | tf_op jit(solution)/shard_map/psum | solution.py:273
  341.9 2.0 broadcast_multiply_fusion
  343.9 1.6 concatenate.50
  345.5 2.2 gather_fusion.3
  (154 shorter events, 37.2 us)
Async XLA Ops:
  7.2 8.5 %copy-start.20 = (s32[1,256]{1,0:T(1,128)S(1)}, s32[1,256]{1,0:T(1,128)}, u32[]{:S(2)}) copy-start(s32[1,256]{1,0:T(1,128)} %param.23) | copy-start | bytes 3076
  7.2 8.5 %copy-start.19 = (s32[1,256]{1,0:T(1,128)S(1)}, s32[1,256]{1,0:T(1,128)}, u32[]{:S(2)}) copy-start(s32[1,256]{1,0:T(1,128)} %param.22) | copy-start | bytes 3076
  7.2 9.9 %copy-start.15 = (bf16[64,16,128]{2,1,0:T(8,128)(2,1)S(1)}, bf16[64,16,128]{2,1,0:T(8,128)(2,1)}, u32[]{:S(2)}) copy-start(bf16[64,16,128]{2,1,0:T(8,128)(2,1)} %param.19) | copy-start | bytes 786436
  7.2 334.7 %all-reduce.19.cloned.1.call-start = ((), (), s32[]{:S(2)}) async-start(), calls=%async_computation.1 | async-start | bytes 1474560 | tf_op jit(solution)/shard_map/psum | solution.py:273
  9.7 7.9 %copy-start.16 = (bf16[64,16,128]{2,1,0:T(8,128)(2,1)S(1)}, bf16[64,16,128]{2,1,0:T(8,128)(2,1)}, u32[]{:S(2)}) copy-start(bf16[64,16,128]{2,1,0:T(8,128)(2,1)} %param.20) | copy-start | bytes 786436
  9.8 11.5 %collective-permute-start = (bf16[80,1,128]{0,2,1:T(8,128)(2,1)S(1)}, bf16[80,1,128]{0,2,1:T(8,128)(2,1)S(1)}, u32[]{:S(2)}, u32[]{:S(2)}) collective-permute-start(bf16[80,1,128]{0,2,1:T(8,128)(2,1)S(1)} %get-tuple-element.99), channel_id=1, source_target_pairs={{0,32},{32,64},{64,96},{96,128},{128,160},{160,192},{192,224},{224... | collective-permute-start | bytes 61448 | tf_op jit(solution)/shard_map/ppermute | solution.py:17
  9.9 11.5 %collective-permute-start.1 = (bf16[80,1,128]{0,2,1:T(8,128)(2,1)S(1)}, bf16[80,1,128]{0,2,1:T(8,128)(2,1)S(1)}, u32[]{:S(2)}, u32[]{:S(2)}) collective-permute-start(bf16[80,1,128]{0,2,1:T(8,128)(2,1)S(1)} %get-tuple-element.100), channel_id=1, source_target_pairs={{32,0},{64,32},{96,64},{128,96},{160,128},{192,160},{224,192},{0,2... | collective-permute-start | bytes 61448 | tf_op jit(solution)/shard_map/ppermute | solution.py:19
  17.5 1.6 copy-start.17
  21.4 15.2 %collective-permute-start.2 = (bf16[80,18,1]{0,2,1:T(2,128)(2,1)S(1)}, bf16[80,18,1]{0,2,1:T(2,128)(2,1)S(1)}, u32[]{:S(2)}, u32[]{:S(2)}) collective-permute-start(bf16[80,18,1]{0,2,1:T(2,128)(2,1)S(1)} %get-tuple-element.97), channel_id=1, source_target_pairs={{0,1},{1,2},{2,3},{3,4},{4,5},{5,6},{6,7},{7,8},{8,9},{9,10},{10,1... | collective-permute-start | bytes 8648 | tf_op jit(solution)/shard_map/ppermute | solution.py:17
  23.1 13.5 %collective-permute-start.3 = (bf16[80,18,1]{0,2,1:T(2,128)(2,1)S(1)}, bf16[80,18,1]{0,2,1:T(2,128)(2,1)S(1)}, u32[]{:S(2)}, u32[]{:S(2)}) collective-permute-start(bf16[80,18,1]{0,2,1:T(2,128)(2,1)S(1)} %get-tuple-element.98), channel_id=1, source_target_pairs={{1,0},{2,1},{3,2},{4,3},{5,4},{6,5},{7,6},{8,7},{9,8},{10,9},{11,1... | collective-permute-start | bytes 8648 | tf_op jit(solution)/shard_map/ppermute | solution.py:19
  63.2 1.0 copy-start.14
  63.2 3.0 copy-start.13
  63.4 2.9 copy-start.12
  64.1 2.2 copy-start.11
  64.2 2.2 copy-start.10
  66.3 1.0 copy-start.18
  66.3 1.0 copy-start.22
  67.2 1.0 copy-start.9
  71.2 1.9 copy-start.6
  71.2 9.8 %copy-start = (bf16[8,64,256]{2,1,0:T(8,128)(2,1)}, bf16[8,64,256]{2,1,0:T(8,128)(2,1)S(1)}, u32[]{:S(2)}) copy-start(bf16[8,64,256]{2,1,0:T(8,128)(2,1)S(1)} %get-tuple-element.84) | copy-start | bytes 786436
  71.2 9.8 %copy-start.2 = (bf16[8,64,256]{2,1,0:T(8,128)(2,1)}, bf16[8,64,256]{2,1,0:T(8,128)(2,1)S(1)}, u32[]{:S(2)}) copy-start(bf16[8,64,256]{2,1,0:T(8,128)(2,1)S(1)} %get-tuple-element.85) | copy-start | bytes 786436
  71.2 9.8 %copy-start.4 = (bf16[8,64,256]{2,1,0:T(8,128)(2,1)}, bf16[8,64,256]{2,1,0:T(8,128)(2,1)S(1)}, u32[]{:S(2)}) copy-start(bf16[8,64,256]{2,1,0:T(8,128)(2,1)S(1)} %get-tuple-element.86) | copy-start | bytes 786436
  75.4 5.7 %copy-start.7 = (bf16[8,64,256]{2,1,0:T(8,128)(2,1)S(1)}, bf16[8,64,256]{2,1,0:T(8,128)(2,1)}, u32[]{:S(2)}) copy-start(bf16[8,64,256]{2,1,0:T(8,128)(2,1)} %copy-done.6) | copy-start | bytes 786436
  75.4 268.5 %all-to-all-start = ((f32[32,64,256]{2,1,0:T(8,128)}), f32[32,64,256]{2,1,0:T(8,128)S(1)}, u32[]{:S(2)}, u32[]{:S(2)}) async-start(f32[32,64,256]{2,1,0:T(8,128)} %broadcast_select_fusion), calls=%async_computation | async-start | bytes 4194304 | tf_op jit(solution)/shard_map/all_to_all | solution.py:268
  105.5 4.8 %copy-start.21 = (pred[16]{0:T(512)(128)(4,1)S(1)}, pred[16]{0:T(512)(128)(4,1)}, u32[]{:S(2)}) copy-start(pred[16]{0:T(512)(128)(4,1)} %constant.228.clone.1) | copy-start | bytes 52
  111.6 4.8 %copy-start.1 = (bf16[8,64,256]{2,1,0:T(8,128)(2,1)S(1)}, bf16[8,64,256]{2,1,0:T(8,128)(2,1)}, u32[]{:S(2)}) copy-start(bf16[8,64,256]{2,1,0:T(8,128)(2,1)} %copy-done) | copy-start | bytes 786436
  111.6 4.8 %copy-start.3 = (bf16[8,64,256]{2,1,0:T(8,128)(2,1)S(1)}, bf16[8,64,256]{2,1,0:T(8,128)(2,1)}, u32[]{:S(2)}) copy-start(bf16[8,64,256]{2,1,0:T(8,128)(2,1)} %copy-done.2) | copy-start | bytes 786436
  111.6 4.7 %copy-start.5 = (bf16[8,64,256]{2,1,0:T(8,128)(2,1)S(1)}, bf16[8,64,256]{2,1,0:T(8,128)(2,1)}, u32[]{:S(2)}) copy-start(bf16[8,64,256]{2,1,0:T(8,128)(2,1)} %copy-done.4) | copy-start | bytes 786436
  111.7 4.7 %copy-start.8 = (bf16[8,64,256]{2,1,0:T(8,128)(2,1)S(1)}, bf16[8,64,256]{2,1,0:T(8,128)(2,1)}, u32[]{:S(2)}) copy-start(bf16[8,64,256]{2,1,0:T(8,128)(2,1)} %copy-done.6) | copy-start | bytes 786436
  112.5 93.1 %collective-permute-start.4 = (f32[64,1,130]{0,2,1:T(8,128)}, f32[64,1,130]{0,2,1:T(8,128)S(1)}, u32[]{:S(2)}, u32[]{:S(2)}) collective-permute-start(f32[64,1,130]{0,2,1:T(8,128)} %get-tuple-element.93), channel_id=1, source_target_pairs={{0,32},{32,64},{64,96},{96,128},{128,160},{160,192},{192,224},{224... | collective-permute-start | bytes 99848 | tf_op jit(solution)/shard_map/ppermute | solution.py:17
  112.5 93.1 %collective-permute-start.5 = (f32[64,1,130]{0,2,1:T(8,128)}, f32[64,1,130]{0,2,1:T(8,128)S(1)}, u32[]{:S(2)}, u32[]{:S(2)}) collective-permute-start(f32[64,1,130]{0,2,1:T(8,128)} %get-tuple-element.94), channel_id=1, source_target_pairs={{32,0},{64,32},{96,64},{128,96},{160,128},{192,160},{224,192},{0,2... | collective-permute-start | bytes 99848 | tf_op jit(solution)/shard_map/ppermute | solution.py:19
  205.6 9.1 %collective-permute-start.7 = (f32[64,20,1]{0,2,1:T(1,128)S(1)}, f32[64,20,1]{0,2,1:T(1,128)S(1)}, u32[]{:S(2)}, u32[]{:S(2)}) collective-permute-start(f32[64,20,1]{0,2,1:T(1,128)S(1)} %get-tuple-element.91), channel_id=1, source_target_pairs={{1,0},{2,1},{3,2},{4,3},{5,4},{6,5},{7,6},{8,7},{9,8},{10,9},{11,1... | collective-permute-start | bytes 15368 | tf_op jit(solution)/shard_map/ppermute | solution.py:19
  206.4 6.7 %collective-permute-start.6 = (f32[64,20,1]{0,2,1:T(1,128)S(1)}, f32[64,20,1]{0,2,1:T(1,128)S(1)}, u32[]{:S(2)}, u32[]{:S(2)}) collective-permute-start(f32[64,20,1]{0,2,1:T(1,128)S(1)} %get-tuple-element.92), channel_id=1, source_target_pairs={{0,1},{1,2},{2,3},{3,4},{4,5},{5,6},{6,7},{7,8},{8,9},{9,10},{10,1... | collective-permute-start | bytes 15368 | tf_op jit(solution)/shard_map/ppermute | solution.py:17
Sparse Core Ops, SparseCore 0:
  73.2 268.5 all-reduce.18
where the time goes:
time: 357 us; the launch traced here: 355 us
  waiting for transfers between devices  125 us (35%)
  local copies, waits for them, and re-layouts  92 us (26%)
  blocking collectives  75.5 us (21%)
  starting transfers between devices  22.7 us (6%)
  other arithmetic  21.3 us (6%)
  between operations  14.7 us (4%)
  matrix products  4.63 us (1%)
    psum x1, waiting for transfers between devices, body(): totals = lax.psum((weight_part, bias_part), ('lat', 'lon'))  120 us
    psum x1, blocking collectives, body(): totals = lax.psum((weight_part, bias_part), ('lat', 'lon'))  75.5 us
    slice x10, local copies, waits for them, and re-layouts, tile_step(): spread[:, row_off * 3 + col_off]  22.7 us
    ppermute x4, starting transfers between devices, extended_2(): lax.ppermute(head, axis, [((i + 1) % count, i) for i in range(count)])  13.9 us
    unnamed x62, local copies, waits for them, and re-layouts  13.4 us
    reshape x9, local copies, waits for them, and re-layouts, tile_step(): tap_list.append(tile_grid[:, :, row_off:row_off + side_cells, col_off:col...  13.1 us
    slice x10, local copies, waits for them, and re-layouts, tile_step(): tile_grid[:, :, row_off:row_off + side_cells, col_off:col_off + side_cells]  11.2 us
  transfers between devices with their start and end apart: 10, of which 2 were waited for; matrix products, arithmetic and copies ran while one was open for 21% of the time, Pallas kernels for 0%

commit v1 on v0

--- a/solution.py
+++ b/solution.py
@@ -270,7 +270,7 @@
     hidden_next = from_tiles(hid_tiles, tile_rows, tile_cols)
     cell_grad = from_tiles(back_tiles, tile_rows, tile_cols)
     hidden_grad = fold_grad(pad_tiles, tile_rows, tile_cols, row_keep)
-    totals = lax.psum((weight_part, bias_part), ("lat", "lon"))
+    totals = lax.psum(lax.psum((weight_part, bias_part), "lon"), "lat")
     scaling = 1.0 / math.sqrt(float(lat_devices * lon_devices * capacity * TILE * TILE))
     return (
         hidden_next,

time: 357 us -> 486 us (1.36)
  waiting for transfers between devices: 125 us -> 243 us
  blocking collectives: 75.5 us -> 85.3 us
    psum x1 -> x2, waiting for transfers between devices: 120 us -> 243 us  [body(): totals = lax.psum(lax.psum((weight_part, bias_part), 'lon'), 'lat')]
    psum x1 -> x2, blocking collectives: 75.5 us -> 85.3 us  [body(): totals = lax.psum(lax.psum((weight_part, bias_part), 'lon'), 'lat')]
  transfers between devices with their start and end apart: 10 -> 11, of which waited for: 2 -> 2; matrix products, arithmetic and copies ran while one was open for 21% -> 15% of each run, Pallas kernels for 0% -> 0%
where the time goes in v1:
time: 486 us; the launch traced here: 484 us
  waiting for transfers between devices  243 us (50%)
  local copies, waits for them, and re-layouts  91.9 us (19%)
  blocking collectives  85.3 us (18%)
  starting transfers between devices  22.9 us (5%)
  other arithmetic  21.2 us (4%)
  between operations  14.7 us (3%)
    psum x2, waiting for transfers between devices, body(): totals = lax.psum(lax.psum((weight_part, bias_part), 'lon'), 'lat')  243 us
    psum x2, blocking collectives, body(): totals = lax.psum(lax.psum((weight_part, bias_part), 'lon'), 'lat')  85.3 us
    slice x10, local copies, waits for them, and re-layouts, tile_step(): spread[:, row_off * 3 + col_off]  22.6 us
    unnamed x62, local copies, waits for them, and re-layouts  13.4 us
    ppermute x4, starting transfers between devices, extended_2(): lax.ppermute(head, axis, [((i + 1) % count, i) for i in range(count)])  13.4 us
    reshape x9, local copies, waits for them, and re-layouts, tile_step(): tap_list.append(tile_grid[:, :, row_off:row_off + side_cells, col_off:col...  13.1 us
    slice x10, local copies, waits for them, and re-layouts, tile_step(): tile_grid[:, :, row_off:row_off + side_cells, col_off:col_off + side_cells]  11.2 us
  transfers between devices with their start and end apart: 11, of which 2 were waited for; matrix products, arithmetic and copies ran while one was open for 15% of the time, Pallas kernels for 0%

profile of v1, /device:TPU:6, one launch (start us, length us, event | category | flops | bytes accessed | tf_op | source)
XLA Modules:
  0.0 483.6 jit_solution(11682873963150306942)
XLA Ops:
  9.9 5.8 %collective-permute-start.1 = (bf16[80,1,128]{0,2,1:T(8,128)(2,1)S(1)}, bf16[80,1,128]{0,2,1:T(8,128)(2,1)S(1)}, u32[]{:S(2)}, u32[]{:S(2)}) collective-permute-start(bf16[80,1,128]{0,2,1:T(8,128)(2,1)S(1)} %get-tuple-element.100), channel_id=1, source_target_pairs={{32,0},{64,32},{96,64},{128,96},{160,128},{192,160},{224,192},{0,2... | collective-permute-start | bytes 61448 | tf_op jit(solution)/shard_map/ppermute | solution.py:19
  21.4 1.7 collective-permute-start.2
  23.1 3.5 collective-permute-start.3
  27.7 1.5 copy.101
  29.3 2.3 copy.109
  31.6 1.5 copy.110
  34.2 2.4 copy.107
  39.1 2.0 fusion.35
  43.2 1.9 copy.88
  45.0 2.0 copy.97
  47.0 1.9 copy.87
  48.9 2.0 copy.96
  50.8 1.9 copy.86
  52.7 2.0 copy.95
  54.7 1.9 copy.85
  56.5 2.0 copy.94
  59.3 2.0 copy.93
  71.3 1.8 convolution_bitcast_fusion.1
  73.8 1.5 broadcast_select_fusion
  75.4 5.6 %all-to-all-start = ((f32[32,64,256]{2,1,0:T(8,128)}), f32[32,64,256]{2,1,0:T(8,128)S(1)}, u32[]{:S(2)}, u32[]{:S(2)}) async-start(f32[32,64,256]{2,1,0:T(8,128)} %broadcast_select_fusion), calls=%async_computation | async-start | bytes 4194304 | tf_op jit(solution)/shard_map/all_to_all | solution.py:268
  81.3 1.7 convolution_bitcast_fusion
  83.1 2.2 fusion.32
  86.7 2.4 copy.120
  89.0 2.4 copy.119
  91.4 2.4 copy.118
  93.7 2.4 copy.117
  96.1 2.4 copy.116
  98.5 2.4 copy.115
  100.9 2.4 copy.114
  103.4 2.3 copy.113
  105.7 4.7 add_bitcast_fusion.1
  112.7 3.9 collective-permute-start.5
  116.8 71.1 %psum.30 = f32[256]{0:T(256)S(1)} all-reduce(f32[256]{0:T(256)S(1)} %convert_reduce_fusion), channel_id=1, replica_groups=mesh['lat'=8,'lon'=32] {'lon'}, use_global_device_ids=true, to_apply=%region_9.10 | all-reduce | flops 256 | bytes 2048 | tf_op jit(solution)/shard_map/psum | solution.py:273
  187.9 14.2 %psum.31 = f32[256]{0:T(256)S(1)} all-reduce(f32[256]{0:T(256)S(1)} %psum.30), channel_id=1, replica_groups=mesh['lat'=8,'lon'=32] {'lat'}, use_global_device_ids=true, to_apply=%region_10.11 | all-reduce | flops 256 | bytes 2048 | tf_op jit(solution)/shard_map/psum | solution.py:273
  202.6 2.0 copy.102
  204.6 1.9 copy.103
  206.5 2.0 copy.126
  208.5 2.3 copy.124
  210.8 2.3 copy.125
  213.2 2.4 copy.128
  215.8 1.9 collective-permute-start.6
  219.0 166.3 %all-reduce.20.cloned.1.call-done = f32[256,720]{0,1:T(8,128)} async-done(((f32[256,720]{0,1:T(8,128)}), f32[256,720]{0,1:T(8,128)}) %all-reduce.20.cloned.1.call-update) | async-done | bytes 737296 | tf_op jit(solution)/shard_map/psum | solution.py:273
  385.3 1.6 scatter-add.14
  387.8 1.6 scatter-add.15
  393.5 76.7 %all-reduce.22.cloned.1.call-done = f32[256,720]{0,1:T(8,128)} async-done(((f32[256,720]{0,1:T(8,128)}), f32[256,720]{0,1:T(8,128)}) %all-reduce.22.cloned.1.call-update) | async-done | bytes 737296 | tf_op jit(solution)/shard_map/psum | solution.py:273
  470.2 2.0 broadcast_multiply_fusion
  472.2 1.6 concatenate.50
  473.8 2.2 gather_fusion.3
  (158 shorter events, 38.5 us)
Async XLA Ops:
  7.2 8.5 %copy-start.20 = (s32[1,256]{1,0:T(1,128)S(1)}, s32[1,256]{1,0:T(1,128)}, u32[]{:S(2)}) copy-start(s32[1,256]{1,0:T(1,128)} %param.23) | copy-start | bytes 3076
  7.2 8.5 %copy-start.19 = (s32[1,256]{1,0:T(1,128)S(1)}, s32[1,256]{1,0:T(1,128)}, u32[]{:S(2)}) copy-start(s32[1,256]{1,0:T(1,128)} %param.22) | copy-start | bytes 3076
  7.2 9.9 %copy-start.15 = (bf16[64,16,128]{2,1,0:T(8,128)(2,1)S(1)}, bf16[64,16,128]{2,1,0:T(8,128)(2,1)}, u32[]{:S(2)}) copy-start(bf16[64,16,128]{2,1,0:T(8,128)(2,1)} %param.19) | copy-start | bytes 786436
  7.2 378.1 %all-reduce.20.cloned.1.call-start = ((), (), s32[]{:S(2)}) async-start(), calls=%async_computation.1 | async-start | bytes 1474560 | tf_op jit(solution)/shard_map/psum | solution.py:273
  9.7 7.9 %copy-start.16 = (bf16[64,16,128]{2,1,0:T(8,128)(2,1)S(1)}, bf16[64,16,128]{2,1,0:T(8,128)(2,1)}, u32[]{:S(2)}) copy-start(bf16[64,16,128]{2,1,0:T(8,128)(2,1)} %param.20) | copy-start | bytes 786436
  9.8 11.5 %collective-permute-start = (bf16[80,1,128]{0,2,1:T(8,128)(2,1)S(1)}, bf16[80,1,128]{0,2,1:T(8,128)(2,1)S(1)}, u32[]{:S(2)}, u32[]{:S(2)}) collective-permute-start(bf16[80,1,128]{0,2,1:T(8,128)(2,1)S(1)} %get-tuple-element.99), channel_id=1, source_target_pairs={{0,32},{32,64},{64,96},{96,128},{128,160},{160,192},{192,224},{224... | collective-permute-start | bytes 61448 | tf_op jit(solution)/shard_map/ppermute | solution.py:17
  9.9 11.5 %collective-permute-start.1 = (bf16[80,1,128]{0,2,1:T(8,128)(2,1)S(1)}, bf16[80,1,128]{0,2,1:T(8,128)(2,1)S(1)}, u32[]{:S(2)}, u32[]{:S(2)}) collective-permute-start(bf16[80,1,128]{0,2,1:T(8,128)(2,1)S(1)} %get-tuple-element.100), channel_id=1, source_target_pairs={{32,0},{64,32},{96,64},{128,96},{160,128},{192,160},{224,192},{0,2... | collective-permute-start | bytes 61448 | tf_op jit(solution)/shard_map/ppermute | solution.py:19
  17.5 1.6 copy-start.17
  21.4 15.2 %collective-permute-start.2 = (bf16[80,18,1]{0,2,1:T(2,128)(2,1)S(1)}, bf16[80,18,1]{0,2,1:T(2,128)(2,1)S(1)}, u32[]{:S(2)}, u32[]{:S(2)}) collective-permute-start(bf16[80,18,1]{0,2,1:T(2,128)(2,1)S(1)} %get-tuple-element.97), channel_id=1, source_target_pairs={{0,1},{1,2},{2,3},{3,4},{4,5},{5,6},{6,7},{7,8},{8,9},{9,10},{10,1... | collective-permute-start | bytes 8648 | tf_op jit(solution)/shard_map/ppermute | solution.py:17
  23.1 13.5 %collective-permute-start.3 = (bf16[80,18,1]{0,2,1:T(2,128)(2,1)S(1)}, bf16[80,18,1]{0,2,1:T(2,128)(2,1)S(1)}, u32[]{:S(2)}, u32[]{:S(2)}) collective-permute-start(bf16[80,18,1]{0,2,1:T(2,128)(2,1)S(1)} %get-tuple-element.98), channel_id=1, source_target_pairs={{1,0},{2,1},{3,2},{4,3},{5,4},{6,5},{7,6},{8,7},{9,8},{10,9},{11,1... | collective-permute-start | bytes 8648 | tf_op jit(solution)/shard_map/ppermute | solution.py:19
  63.2 1.0 copy-start.14
  63.2 3.0 copy-start.13
  63.4 2.9 copy-start.12
  64.2 2.2 copy-start.11
  64.2 2.2 copy-start.10
  66.3 1.0 copy-start.18
  66.3 1.0 copy-start.22
  67.3 1.0 copy-start.9
  71.2 1.9 copy-start.6
  71.2 10.0 %copy-start = (bf16[8,64,256]{2,1,0:T(8,128)(2,1)}, bf16[8,64,256]{2,1,0:T(8,128)(2,1)S(1)}, u32[]{:S(2)}) copy-start(bf16[8,64,256]{2,1,0:T(8,128)(2,1)S(1)} %get-tuple-element.84) | copy-start | bytes 786436
  71.2 10.0 %copy-start.2 = (bf16[8,64,256]{2,1,0:T(8,128)(2,1)}, bf16[8,64,256]{2,1,0:T(8,128)(2,1)S(1)}, u32[]{:S(2)}) copy-start(bf16[8,64,256]{2,1,0:T(8,128)(2,1)S(1)} %get-tuple-element.85) | copy-start | bytes 786436
  71.2 10.0 %copy-start.4 = (bf16[8,64,256]{2,1,0:T(8,128)(2,1)}, bf16[8,64,256]{2,1,0:T(8,128)(2,1)S(1)}, u32[]{:S(2)}) copy-start(bf16[8,64,256]{2,1,0:T(8,128)(2,1)S(1)} %get-tuple-element.86) | copy-start | bytes 786436
  75.4 5.9 %copy-start.7 = (bf16[8,64,256]{2,1,0:T(8,128)(2,1)S(1)}, bf16[8,64,256]{2,1,0:T(8,128)(2,1)}, u32[]{:S(2)}) copy-start(bf16[8,64,256]{2,1,0:T(8,128)(2,1)} %copy-done.6) | copy-start | bytes 786436
  75.4 396.9 %all-to-all-start = ((f32[32,64,256]{2,1,0:T(8,128)}), f32[32,64,256]{2,1,0:T(8,128)S(1)}, u32[]{:S(2)}, u32[]{:S(2)}) async-start(f32[32,64,256]{2,1,0:T(8,128)} %broadcast_select_fusion), calls=%async_computation | async-start | bytes 4194304 | tf_op jit(solution)/shard_map/all_to_all | solution.py:268
  81.0 389.2 %all-reduce.22.cloned.1.call-start = ((), (), s32[]{:S(2)}) async-start(), calls=%async_computation.2 | async-start | bytes 1474560 | tf_op jit(solution)/shard_map/psum | solution.py:273
  105.7 4.7 copy-start.21
  111.8 4.8 copy-start.1
  111.8 4.8 copy-start.3
  111.8 4.7 copy-start.5
  111.8 4.7 copy-start.8
  112.7 102.8 %collective-permute-start.4 = (f32[64,1,130]{0,2,1:T(8,128)}, f32[64,1,130]{0,2,1:T(8,128)S(1)}, u32[]{:S(2)}, u32[]{:S(2)}) collective-permute-start(f32[64,1,130]{0,2,1:T(8,128)} %get-tuple-element.93), channel_id=1, source_target_pairs={{0,32},{32,64},{64,96},{96,128},{128,160},{160,192},{192,224},{224... | collective-permute-start | bytes 99848 | tf_op jit(solution)/shard_map/ppermute | solution.py:17
  112.7 102.8 %collective-permute-start.5 = (f32[64,1,130]{0,2,1:T(8,128)}, f32[64,1,130]{0,2,1:T(8,128)S(1)}, u32[]{:S(2)}, u32[]{:S(2)}) collective-permute-start(f32[64,1,130]{0,2,1:T(8,128)} %get-tuple-element.94), channel_id=1, source_target_pairs={{32,0},{64,32},{96,64},{128,96},{160,128},{192,160},{224,192},{0,2... | collective-permute-start | bytes 99848 | tf_op jit(solution)/shard_map/ppermute | solution.py:19
  215.6 171.3 %collective-permute-start.7 = (f32[64,20,1]{0,2,1:T(1,128)S(1)}, f32[64,20,1]{0,2,1:T(1,128)S(1)}, u32[]{:S(2)}, u32[]{:S(2)}) collective-permute-start(f32[64,20,1]{0,2,1:T(1,128)S(1)} %get-tuple-element.91), channel_id=1, source_target_pairs={{1,0},{2,1},{3,2},{4,3},{5,4},{6,5},{7,6},{8,7},{9,8},{10,9},{11,1... | collective-permute-start | bytes 15368 | tf_op jit(solution)/shard_map/ppermute | solution.py:19
  215.8 169.5 %collective-permute-start.6 = (f32[64,20,1]{0,2,1:T(1,128)S(1)}, f32[64,20,1]{0,2,1:T(1,128)S(1)}, u32[]{:S(2)}, u32[]{:S(2)}) collective-permute-start(f32[64,20,1]{0,2,1:T(1,128)S(1)} %get-tuple-element.92), channel_id=1, source_target_pairs={{0,1},{1,2},{2,3},{3,4},{4,5},{5,6},{6,7},{7,8},{8,9},{9,10},{10,1... | collective-permute-start | bytes 15368 | tf_op jit(solution)/shard_map/ppermute | solution.py:17
Sparse Core Ops, SparseCore 0:
  73.2 311.9 all-reduce.19
  387.9 82.2 all-reduce.21
